TPU v7x, 32 devices: a whole 2x2x4 slice. The times are simulated.
32 devices in a mesh: row: 8 (over y, x, core), col: 4 (over z).
Axes of the slice: x: 2, y: 2, z: 4, core: 2. Of those that a mesh axis runs over, the one named last changes fastest.
Arguments:
- solution: float32 [64, 32768], P(None, ('row', 'col')), may hold values from -6 to 6
- residual: float32 [64, 65536], P(None, ('row', 'col')), may hold values from -6 to 6
- direction: float32 [64, 32768], P(None, ('row', 'col')), may hold values from -6 to 6
- jacobian_tiles: bfloat16 [512, 20, 128, 128], P('row', 'col'), may hold values from -0.125 to 0.125
- tile_blocks: int32 [512, 20], P('row', 'col'), may hold values from 0 to 63, as said below
- tile_counts: int32 [512, 4], P('row', 'col'), may hold values from 1 to 5, as said below
Outputs:
- solution_next: float32 [64, 32768], P(None, ('row', 'col'))
- residual_next: float32 [64, 65536], P(None, ('row', 'col'))
- direction_next: float32 [64, 32768], P(None, ('row', 'col'))
Inputs may be any that keep to these rules, and one draw needn't show every extreme that they name: `tile_blocks`: within each sensor and parameter group the 5 entries are different. Only the first tile_counts[i, c] slots of sensor i in group c hold a tile; some sensor fills all 5 slots of every group.
All inputs are finite; a program needn't handle non-finite values.
Results may differ from a plain program's by a relative error of at most 0.023.
Values may be sent and summed in bfloat16 or wider, within the bound.
No kernel may reach another device: no remote copies, remote signals or barrier semaphores. Data moves between devices by JAX's collectives and lax.ppermute only.
A program may use at most 128 MiB of HBM per device.

v0:
```python
import jax
import jax.numpy as jnp
from jax import lax
from jax.sharding import PartitionSpec as P

CB_DEV = 64
ITERS = 2


def times_highest(left, right):
    return jnp.dot(left, right, precision=lax.Precision.HIGHEST)


def gram_matrix(values):
    return jnp.dot(values, values.T, precision=lax.Precision.HIGHEST)


def solve_spd(matrix, right):
    factor_low = jnp.linalg.cholesky(matrix)
    middle = lax.linalg.triangular_solve(factor_low, right, left_side=True, lower=True)
    return lax.linalg.triangular_solve(
        factor_low, middle, left_side=True, lower=True, transpose_a=True
    )


def images(jacobian_tiles, tile_blocks, live_slot, direction_half):
    rhs_count = direction_half.shape[0]
    tile_width = jacobian_tiles.shape[2]
    table_view = direction_half.reshape(rhs_count, -1, tile_width)
    picked = jnp.take(table_view, tile_blocks, axis=1) * live_slot[None, :, :, None]
    product = jnp.einsum(
        "rsab,nrsb->nra", jacobian_tiles, picked, preferred_element_type=jnp.float32
    )
    return product.reshape(rhs_count, -1)


def gradients(jacobian_tiles, tile_blocks, live_slot, rows_half):
    rhs_count = rows_half.shape[0]
    tile_width = jacobian_tiles.shape[2]
    sensors = jacobian_tiles.shape[0]
    row_view = rows_half.reshape(rhs_count, sensors, tile_width)
    contrib = jnp.einsum(
        "rsab,nra->rsnb", jacobian_tiles, row_view, preferred_element_type=jnp.float32
    )
    contrib = contrib * live_slot.astype(jnp.float32)[:, :, None, None]
    summed = jax.ops.segment_sum(
        contrib.reshape(-1, rhs_count, tile_width), tile_blocks.reshape(-1), num_segments=CB_DEV
    )
    return summed.transpose(1, 0, 2).reshape(rhs_count, CB_DEV * tile_width)


def per_device(solution, residual, direction, jacobian_tiles, tile_blocks, tile_counts):
    live_slot = (
        jnp.arange(jacobian_tiles.shape[1], dtype=jnp.int32)[None, :] < tile_counts
    ).astype(jnp.bfloat16)
    share_rows = residual.shape[1]
    col_start = lax.axis_index("col") * share_rows
    rows_now = lax.all_gather(residual.astype(jnp.bfloat16), "col", axis=1, tiled=True).astype(
        residual.dtype
    )

    def gradient_step(rows_value):
        rows_half = rows_value.astype(jnp.bfloat16)
        partial_term = gradients(jacobian_tiles, tile_blocks, live_slot, rows_half)
        gradient = lax.psum_scatter(
            partial_term.astype(jnp.bfloat16), "row", scatter_dimension=1, tiled=True
        ).astype(jnp.float32)
        gamma_value = lax.psum(gram_matrix(gradient), ("row", "col"))
        return (gradient, gamma_value)

    gradient, gamma_now = gradient_step(rows_now)
    iterate = solution
    for iteration in range(ITERS):
        direction_half = lax.all_gather(direction.astype(jnp.bfloat16), "row", axis=1, tiled=True)
        image_partial_term = images(jacobian_tiles, tile_blocks, live_slot, direction_half)
        image = lax.psum(image_partial_term.astype(jnp.bfloat16), "col").astype(jnp.float32)
        curvature = lax.psum(gram_matrix(image), "row")
        image, curvature = (image, curvature)
        step_alpha = solve_spd(curvature, gamma_now)
        iterate = iterate + times_highest(step_alpha.T, direction)
        rows_now = rows_now - times_highest(step_alpha.T, image)
        gradient, gamma_next = gradient_step(rows_now)
        step_beta = solve_spd(gamma_now, gamma_next)
        direction = gradient + times_highest(step_beta.T, direction)
        gamma_now = gamma_next
    residual_out = lax.dynamic_slice_in_dim(rows_now, col_start, share_rows, 1)
    return (iterate, residual_out, direction)


def solution(mesh):
    placed = (
        P(None, ("row", "col")),
        P(None, ("row", "col")),
        P(None, ("row", "col")),
        P("row", "col", None, None),
        P("row", "col"),
        P("row", "col"),
    )
    return jax.shard_map(
        per_device,
        mesh=mesh,
        in_specs=placed,
        out_specs=(P(None, ("row", "col")), P(None, ("row", "col")), P(None, ("row", "col"))),
        check_vma=False,
    )
```

profile of v0, /device:TPU:0, one launch (start us, length us, event | category | flops | bytes accessed | tf_op | source)
XLA Modules:
  0.0 650.2 jit_solution(2488741487716216295)
XLA Ops:
  14.2 26.7 %all-gather.6.cloned.1.call-done = bf16[64,8192]{1,0:T(8,128)(2,1)} async-done(((bf16[64,2048]{1,0:T(8,128)(2,1)}), bf16[64,8192]{1,0:T(8,128)(2,1)}) %all-gather.6.cloned.1.call-update) | async-done | bytes 1048592 | tf_op jit(solution)/shard_map/all_gather | solution.py:58
  42.4 10.2 %broadcast_multiply_fusion.2 = f32[64,64,5,128]{3,1,2,0:T(8,128)} fusion(f32[64,5]{1,0:T(8,128)S(1)} %get-tuple-element.8, bf16[64,5,128,128]{3,2,1,0:T(8,128)(2,1)} %param.16, bf16[64,64,128,1]{2,1,0,3:T(8,128)(2,1)S(1)} %bitcast.184), kind=kOutput, calls=%fused_computation.15 | convolution fusion | flops 673710080 | bytes 22021376 | tf_op jit(solution)/shard_map/rsab,nra->rsnb/dot_general | solution.py:42
  52.8 33.0 %scatter_fusion = f32[64,64,128]{2,1,0:T(8,128)S(1)} fusion(f32[64,64,128]{2,1,0:T(8,128)S(1)} %broadcast.76.clone, s32[320]{0:T(512)S(1)} %reshape.148, f32[320,64,128]{2,1,0:T(8,128)} %bitcast.178), kind=kCustom, calls=%fused_computation.2 | custom fusion | flops 2621440 | bytes 31458560 | tf_op jit(solution)/shard_map/scatter-add | solution.py:46
  87.3 13.3 %gather_fusion = bf16[320,64,128]{2,1,0:T(8,128)(2,1)} fusion(bf16[64,64,128]{2,0,1:T(8,128)(2,1)S(1)} %copy_bitcast_fusion.6, s32[1024]{0:T(1024)S(1)} %pad_clamp_fusion), kind=kCustom, calls=%fused_computation.clone | custom fusion | bytes 10487040 | tf_op jit(solution)/shard_map/jit(_take)/gather | solution.py:30
  100.7 11.0 %fusion.10 = bf16[64,8,8,128]{3,2,1,0:T(8,128)(2,1)} fusion(bf16[64,5,128,128]{3,2,1,0:T(8,128)(2,1)} %param.16, bf16[64,5,64,128]{3,2,1,0:T(8,128)(2,1)} %bitcast.181, pred[64,5]{1,0:T(8,128)(4,1)S(1)} %copy.44, bf16[64,5]{1,0:T(8,128)(2,1)S(1)} %get-tuple-element.6), kind=kOutput, calls=%fused_computation.24 | convolution fusion | flops 676855808 | bytes 16778176 | tf_op jit(solution)/shard_map/rsab,nrsb->nra/dot_general | solution.py:31
  111.7 2.5 copy.106
  116.0 49.8 %all-reduce.3.cloned.1.call-done = bf16[64,8192]{1,0:T(8,128)(2,1)} async-done(((bf16[64,8192]{1,0:T(8,128)(2,1)}), bf16[64,8192]{1,0:T(8,128)(2,1)}) %all-reduce.3.cloned.1.call-update) | async-done | bytes 1048592 | tf_op jit(solution)/shard_map/psum | solution.py:76
  167.7 24.2 %psum.50 = f32[64,64]{0,1:T(8,128)S(1)} all-reduce(f32[64,64]{0,1:T(8,128)S(1)} %fusion.44), channel_id=1, replica_groups=mesh['row'=8,'col'=4] {'row'}, use_global_device_ids=true, to_apply=%region_1.3 | all-reduce | flops 4096 | bytes 32768 | tf_op jit(solution)/shard_map/psum | solution.py:77
  192.0 5.8 cholesky.74
  199.2 4.9 custom-call.15
  205.3 39.4 %psum.51 = f32[64,64]{0,1:T(8,128)S(1)} all-reduce(f32[64,64]{0,1:T(8,128)S(1)} %fusion.45), channel_id=1, replica_groups=mesh['row'=8,'col'=4] {'row','col'}, use_global_device_ids=true, to_apply=%region_6.9 | all-reduce | flops 4096 | bytes 32768 | tf_op jit(solution)/shard_map/psum | solution.py:68
  245.1 2.3 convolution_subtract_fusion.1
  249.2 10.2 %broadcast_multiply_fusion.1 = f32[64,64,5,128]{3,1,2,0:T(8,128)} fusion(f32[64,5]{1,0:T(8,128)S(1)} %get-tuple-element.8, bf16[64,5,128,128]{3,2,1,0:T(8,128)(2,1)} %param.16, bf16[64,64,128,1]{2,1,0,3:T(8,128)(2,1)S(1)} %bitcast.183), kind=kOutput, calls=%fused_computation.14 | convolution fusion | flops 673710080 | bytes 22021376 | tf_op jit(solution)/shard_map/rsab,nra->rsnb/dot_general | solution.py:42
  259.6 33.0 %scatter_fusion.1 = f32[64,64,128]{2,1,0:T(8,128)S(1)} fusion(f32[64,64,128]{2,1,0:T(8,128)S(1)} %broadcast.76.clone.1, s32[320]{0:T(512)S(1)} %reshape.148, f32[320,64,128]{2,1,0:T(8,128)} %bitcast.179), kind=kCustom, calls=%fused_computation.3 | custom fusion | flops 2621440 | bytes 31458560 | tf_op jit(solution)/shard_map/scatter-add | solution.py:46
  293.9 5.8 cholesky.85
  301.1 4.9 custom-call.17
  305.9 24.9 %reduce-scatter.6.cloned.1.call-done = bf16[64,1024]{1,0:T(8,128)(2,1)} async-done(((bf16[64,8192]{1,0:T(8,128)(2,1)}), bf16[64,1024]{1,0:T(8,128)(2,1)}) %reduce-scatter.6.cloned.1.call-update) | async-done | bytes 131088 | tf_op jit(solution)/shard_map/reduce_scatter | solution.py:65
  332.0 39.4 %psum.52 = f32[64,64]{0,1:T(8,128)S(1)} all-reduce(f32[64,64]{0,1:T(8,128)S(1)} %fusion.46), channel_id=1, replica_groups=mesh['row'=8,'col'=4] {'row','col'}, use_global_device_ids=true, to_apply=%region_9.14 | all-reduce | flops 4096 | bytes 32768 | tf_op jit(solution)/shard_map/psum | solution.py:68
  374.1 24.1 %all-gather.8.cloned.1.call-done = bf16[64,8192]{1,0:T(8,128)(2,1)} async-done(((bf16[64,1024]{1,0:T(8,128)(2,1)}), bf16[64,8192]{1,0:T(8,128)(2,1)}) %all-gather.8.cloned.1.call-update) | async-done | bytes 1048592 | tf_op jit(solution)/shard_map/all_gather | solution.py:74
  399.7 13.3 %gather_fusion.1 = bf16[320,64,128]{2,1,0:T(8,128)(2,1)} fusion(bf16[64,64,128]{2,0,1:T(8,128)(2,1)S(1)} %copy_bitcast_fusion.5, s32[1024]{0:T(1024)S(1)} %pad_clamp_fusion), kind=kCustom, calls=%fused_computation.1.clone | custom fusion | bytes 10487040 | tf_op jit(solution)/shard_map/jit(_take)/gather | solution.py:30
  413.1 11.0 %fusion.11 = bf16[64,8,8,128]{3,2,1,0:T(8,128)(2,1)} fusion(bf16[64,5,128,128]{3,2,1,0:T(8,128)(2,1)} %param.16, bf16[64,5,64,128]{3,2,1,0:T(8,128)(2,1)} %bitcast.180, pred[64,5]{1,0:T(8,128)(4,1)S(1)} %copy.44, bf16[64,5]{1,0:T(8,128)(2,1)S(1)} %get-tuple-element.6), kind=kOutput, calls=%fused_computation.25 | convolution fusion | flops 676855808 | bytes 16778176 | tf_op jit(solution)/shard_map/rsab,nrsb->nra/dot_general | solution.py:31
  424.1 2.6 copy.105
  426.8 52.0 %all-reduce.5.cloned.1.call-done = bf16[64,8192]{1,0:T(8,128)(2,1)} async-done(((bf16[64,8192]{1,0:T(8,128)(2,1)}), bf16[64,8192]{1,0:T(8,128)(2,1)}) %all-reduce.5.cloned.1.call-update) | async-done | bytes 1048592 | tf_op jit(solution)/shard_map/psum | solution.py:76
  480.8 24.4 %psum.54 = f32[64,64]{0,1:T(8,128)S(1)} all-reduce(f32[64,64]{0,1:T(8,128)S(1)} %fusion.47), channel_id=1, replica_groups=mesh['row'=8,'col'=4] {'row'}, use_global_device_ids=true, to_apply=%region_11.16 | all-reduce | flops 4096 | bytes 32768 | tf_op jit(solution)/shard_map/psum | solution.py:77
  505.3 5.8 cholesky.96
  512.5 4.9 custom-call.19
  521.9 10.2 %broadcast_multiply_fusion = f32[64,64,5,128]{3,1,2,0:T(8,128)} fusion(f32[64,5]{1,0:T(8,128)S(1)} %get-tuple-element.8, bf16[64,5,128,128]{3,2,1,0:T(8,128)(2,1)} %param.16, bf16[64,64,128,1]{2,1,0,3:T(8,128)(2,1)S(1)} %bitcast.182), kind=kOutput, calls=%fused_computation.13 | convolution fusion | flops 673710080 | bytes 22021376 | tf_op jit(solution)/shard_map/rsab,nra->rsnb/dot_general | solution.py:42
  532.3 33.0 %scatter_fusion.2 = f32[64,64,128]{2,1,0:T(8,128)S(1)} fusion(f32[64,64,128]{2,1,0:T(8,128)S(1)} %broadcast.76, s32[320]{0:T(512)S(1)} %reshape.148, f32[320,64,128]{2,1,0:T(8,128)} %bitcast.177), kind=kCustom, calls=%fused_computation.4 | custom fusion | flops 2621440 | bytes 31458560 | tf_op jit(solution)/shard_map/scatter-add | solution.py:46
  566.9 5.8 cholesky.107
  574.1 4.9 custom-call.21
  582.0 18.1 %reduce-scatter.8.cloned.1.call-done = bf16[64,1024]{1,0:T(8,128)(2,1)} async-done(((bf16[64,8192]{1,0:T(8,128)(2,1)}), bf16[64,1024]{1,0:T(8,128)(2,1)}) %reduce-scatter.8.cloned.1.call-update) | async-done | bytes 131088 | tf_op jit(solution)/shard_map/reduce_scatter | solution.py:65
  601.3 39.4 %psum.55 = f32[64,64]{1,0:T(8,128)S(1)} all-reduce(f32[64,64]{1,0:T(8,128)S(1)} %fusion.48), channel_id=1, replica_groups=mesh['row'=8,'col'=4] {'row','col'}, use_global_device_ids=true, to_apply=%region_14.19 | all-reduce | flops 4096 | bytes 32768 | tf_op jit(solution)/shard_map/psum | solution.py:68
  (93 shorter events, 44.3 us)
Async XLA Ops:
  7.2 33.7 %all-gather.6.cloned.1.call-start = ((), (), s32[]{:S(2)}) async-start(), calls=%async_computation.5 | async-start | bytes 1310720 | tf_op jit(solution)/shard_map/all_gather | solution.py:58
  9.0 76.8 %all-gather.4.cloned.1.call-start = ((), (), s32[]{:S(2)}) async-start(), calls=%async_computation.3 | async-start | bytes 1179648 | tf_op jit(solution)/shard_map/all_gather | solution.py:74
  10.7 155.0 %all-reduce.3.cloned.1.call-start = ((), (), s32[]{:S(2)}) async-start(), calls=%async_computation.4 | async-start | bytes 2097152 | tf_op jit(solution)/shard_map/psum | solution.py:76
  111.7 133.4 %copy-start.3 = (bf16[64,8192]{1,0:T(8,128)(2,1)S(1)}, bf16[64,8192]{1,0:T(8,128)(2,1)}, u32[]{:S(2)}) copy-start(bf16[64,8192]{1,0:T(8,128)(2,1)} %all-gather.6.cloned.1.call-done) | copy-start | bytes 3145732
  114.3 89.9 %reduce-scatter.4.cloned.1.call-start = ((), (), s32[]{:S(2)}) async-start(), calls=%async_computation.6 | async-start | bytes 1179648 | tf_op jit(solution)/shard_map/reduce_scatter | solution.py:65
  115.4 215.4 %reduce-scatter.6.cloned.1.call-start = ((), (), s32[]{:S(2)}) async-start(), calls=%async_computation.7 | async-start | bytes 1179648 | tf_op jit(solution)/shard_map/reduce_scatter | solution.py:65
  247.4 1.3 copy-start
  259.6 112.3 %copy-start.4 = (f32[64,1024]{1,0:T(8,128)S(1)}, f32[64,1024]{1,0:T(8,128)}, u32[]{:S(2)}) copy-start(f32[64,1024]{1,0:T(8,128)} %param.15) | copy-start | bytes 786436
  293.7 104.5 %all-gather.8.cloned.1.call-start = ((), (), s32[]{:S(2)}) async-start(), calls=%async_computation.8 | async-start | bytes 1179648 | tf_op jit(solution)/shard_map/all_gather | solution.py:74
  373.9 104.9 %all-reduce.5.cloned.1.call-start = ((), (), s32[]{:S(2)}) async-start(), calls=%async_computation.9 | async-start | bytes 2097152 | tf_op jit(solution)/shard_map/psum | solution.py:76
  424.1 93.7 %copy-start.1 = (f32[64,8192]{1,0:T(8,128)S(1)}, f32[64,8192]{1,0:T(8,128)}, u32[]{:S(2)}) copy-start(f32[64,8192]{1,0:T(8,128)} %copy-done) | copy-start | bytes 6291460
  426.7 173.4 %reduce-scatter.8.cloned.1.call-start = ((), (), s32[]{:S(2)}) async-start(), calls=%async_computation.10 | async-start | bytes 1179648 | tf_op jit(solution)/shard_map/reduce_scatter | solution.py:65
  520.1 1.3 copy-start.2
  532.3 34.2 %copy-start.5 = (f32[64,1024]{1,0:T(8,128)S(1)}, f32[64,1024]{1,0:T(8,128)}, u32[]{:S(2)}) copy-start(f32[64,1024]{1,0:T(8,128)} %param.13) | copy-start | bytes 786436
Sparse Core Ops, SparseCore 0:
  10.1 30.6 all-gather.5
  43.3 22.7 all-gather.3
  114.4 51.2 all-reduce.2
  168.7 35.3 reduce-scatter.3
  293.8 36.9 reduce-scatter.5
  374.0 24.1 all-gather.7
  426.9 51.8 all-reduce.4
  566.5 33.5 reduce-scatter.7
where the time goes:
time: 662 us; the launch traced here: 650 us
  waiting for transfers between devices  196 us (30%)
  blocking collectives  167 us (25%)
  other arithmetic  156 us (24%)
  matrix products  71.7 us (11%)
  local copies, waits for them, and re-layouts  43.6 us (7%)
  between operations  14.8 us (2%)
    psum x3, blocking collectives, gradient_step(): gamma_value = lax.psum(gram_matrix(gradient), ('row', 'col'))  118 us
    psum x2, waiting for transfers between devices, per_device(): lax.psum(image_partial_term.astype(jnp.bfloat16), 'col').astype(jnp.float32)  102 us
    scatter-add x3, other arithmetic, gradients(): jax.ops.segment_sum(contrib.reshape(-1, rhs_count, tile_width), tile_bloc...  99 us
    psum x2, blocking collectives, per_device(): curvature = lax.psum(gram_matrix(image), 'row')  48.6 us
    reduce_scatter x3, waiting for transfers between devices, gradient_step(): lax.psum_scatter(partial_term.astype(jnp.bfloat16), 'row', scatter_dimens...  43.1 us
    dot_general x3, matrix products, gradients(): jnp.einsum('rsab,nra->rsnb', jacobian_tiles, row_view, preferred_element_...  30.5 us
    all_gather x1, waiting for transfers between devices, per_device(): lax.all_gather(residual.astype(jnp.bfloat16), 'col', axis=1, tiled=True)  26.7 us
    gather x2, local copies, waits for them, and re-layouts, images(): jnp.take(table_view, tile_blocks, axis=1) * live_slot[None, :, :, None]  26.7 us
  transfers between devices with their start and end apart: 8, of which 7 were waited for; matrix products, arithmetic and copies ran while one was open for 14% of the time, Pallas kernels for 0%

commit v1 on v0

--- a/solution.py
+++ b/solution.py
@@ -65,7 +65,7 @@
         gradient = lax.psum_scatter(
             partial_term.astype(jnp.bfloat16), "row", scatter_dimension=1, tiled=True
         ).astype(jnp.float32)
-        gamma_value = lax.psum(gram_matrix(gradient), ("row", "col"))
+        gamma_value = jnp.sum(lax.all_gather(gram_matrix(gradient), ("row", "col")), axis=0)
         return (gradient, gamma_value)
 
     gradient, gamma_now = gradient_step(rows_now)

time: 662 us -> 762 us (1.15)
  blocking collectives: 167 us -> 277 us
    all_gather x0 -> x3, blocking collectives: none -> 229 us  [gradient_step(): lax.all_gather(gram_matrix(gradient), ('row', 'col'))]
    psum x3 -> x0, blocking collectives: 118 us -> none  [gradient_step(): gamma_value = lax.psum(gram_matrix(gradient), ('row', 'col'))]
  transfers between devices with their start and end apart: 8 -> 8, of which waited for: 7 -> 6; matrix products, arithmetic and copies ran while one was open for 14% -> 12% of each run, Pallas kernels for 0% -> 0%
where the time goes in v1:
time: 762 us; the launch traced here: 750 us
  blocking collectives  277 us (36%)
  waiting for transfers between devices  189 us (25%)
  other arithmetic  157 us (21%)
  matrix products  69.5 us (9%)
  local copies, waits for them, and re-layouts  42.3 us (6%)
  between operations  14.8 us (2%)
    all_gather x3, blocking collectives, gradient_step(): lax.all_gather(gram_matrix(gradient), ('row', 'col'))  229 us
    psum x2, waiting for transfers between devices, per_device(): lax.psum(image_partial_term.astype(jnp.bfloat16), 'col').astype(jnp.float32)  102 us
    scatter-add x3, other arithmetic, gradients(): jax.ops.segment_sum(contrib.reshape(-1, rhs_count, tile_width), tile_bloc...  99 us
    psum x2, blocking collectives, per_device(): curvature = lax.psum(gram_matrix(image), 'row')  48.6 us
    reduce_scatter x3, waiting for transfers between devices, gradient_step(): lax.psum_scatter(partial_term.astype(jnp.bfloat16), 'row', scatter_dimens...  39.5 us
    dot_general x3, matrix products, gradients(): jnp.einsum('rsab,nra->rsnb', jacobian_tiles, row_view, preferred_element_...  30.5 us
    all_gather x1, waiting for transfers between devices, per_device(): lax.all_gather(residual.astype(jnp.bfloat16), 'col', axis=1, tiled=True)  26.7 us
    gather x2, local copies, waits for them, and re-layouts, images(): jnp.take(table_view, tile_blocks, axis=1) * live_slot[None, :, :, None]  26.7 us
  transfers between devices with their start and end apart: 8, of which 6 were waited for; matrix products, arithmetic and copies ran while one was open for 12% of the time, Pallas kernels for 0%

profile of v1, /device:TPU:0, one launch (start us, length us, event | category | flops | bytes accessed | tf_op | source)
XLA Modules:
  0.0 750.3 jit_solution(7412588432575185843)
XLA Ops:
  14.2 26.7 %all-gather.9.cloned.1.call-done = bf16[64,8192]{1,0:T(8,128)(2,1)} async-done(((bf16[64,2048]{1,0:T(8,128)(2,1)}), bf16[64,8192]{1,0:T(8,128)(2,1)}) %all-gather.9.cloned.1.call-update) | async-done | bytes 1048592 | tf_op jit(solution)/shard_map/all_gather | solution.py:58
  42.4 10.2 %broadcast_multiply_fusion.2 = f32[64,64,5,128]{3,1,2,0:T(8,128)} fusion(f32[64,5]{1,0:T(8,128)S(1)} %get-tuple-element.8, bf16[64,5,128,128]{3,2,1,0:T(8,128)(2,1)} %param.16, bf16[64,64,128,1]{2,1,0,3:T(8,128)(2,1)S(1)} %bitcast.187), kind=kOutput, calls=%fused_computation.15 | convolution fusion | flops 673710080 | bytes 22021376 | tf_op jit(solution)/shard_map/rsab,nra->rsnb/dot_general | solution.py:42
  52.8 33.0 %scatter_fusion = f32[64,64,128]{2,1,0:T(8,128)S(1)} fusion(f32[64,64,128]{2,1,0:T(8,128)S(1)} %broadcast.76.clone, s32[320]{0:T(512)S(1)} %reshape.148, f32[320,64,128]{2,1,0:T(8,128)} %bitcast.181), kind=kCustom, calls=%fused_computation.2 | custom fusion | flops 2621440 | bytes 31458560 | tf_op jit(solution)/shard_map/scatter-add | solution.py:46
  87.3 13.3 %gather_fusion = bf16[320,64,128]{2,1,0:T(8,128)(2,1)} fusion(bf16[64,64,128]{2,0,1:T(8,128)(2,1)S(1)} %copy_bitcast_fusion.6, s32[1024]{0:T(1024)S(1)} %pad_clamp_fusion), kind=kCustom, calls=%fused_computation.clone | custom fusion | bytes 10487040 | tf_op jit(solution)/shard_map/jit(_take)/gather | solution.py:30
  100.7 10.0 %fusion.10 = bf16[64,8,8,128]{3,2,1,0:T(8,128)(2,1)S(1)} fusion(bf16[64,5,128,128]{3,2,1,0:T(8,128)(2,1)} %param.16, bf16[64,5,64,128]{3,2,1,0:T(8,128)(2,1)} %bitcast.184, pred[64,5]{1,0:T(8,128)(4,1)S(1)} %copy.61, bf16[64,5]{1,0:T(8,128)(2,1)S(1)} %get-tuple-element.6), kind=kOutput, calls=%fused_computation.24 | convolution fusion | flops 676855808 | bytes 16778176 | tf_op jit(solution)/shard_map/rsab,nrsb->nra/dot_general | solution.py:31
  113.6 49.8 %all-reduce.3.cloned.1.call-done = bf16[64,8192]{1,0:T(8,128)(2,1)} async-done(((bf16[64,8192]{1,0:T(8,128)(2,1)}), bf16[64,8192]{1,0:T(8,128)(2,1)}) %all-reduce.3.cloned.1.call-update) | async-done | bytes 1048592 | tf_op jit(solution)/shard_map/psum | solution.py:76
  163.4 2.0 fusion.44
  165.4 24.2 %psum.29 = f32[64,64]{0,1:T(8,128)S(1)} all-reduce(f32[64,64]{0,1:T(8,128)S(1)} %fusion.44), channel_id=1, replica_groups=mesh['row'=8,'col'=4] {'row'}, use_global_device_ids=true, to_apply=%region_1.3 | all-reduce | flops 4096 | bytes 32768 | tf_op jit(solution)/shard_map/psum | solution.py:77
  189.7 5.8 cholesky.74
  196.9 4.9 custom-call.15
  203.0 76.0 %all-gather = f32[2048,64]{1,0:T(8,128)S(1)} all-gather(f32[64,64]{1,0:T(8,128)S(1)} %fusion.45), channel_id=2, replica_groups=mesh['row'=8,'col'=4] {'row','col'}, dimensions={0}, use_global_device_ids=true | all-gather | bytes 540672 | tf_op jit(solution)/shard_map/all_gather | solution.py:68
  282.4 10.2 %broadcast_multiply_fusion.1 = f32[64,64,5,128]{3,1,2,0:T(8,128)} fusion(f32[64,5]{1,0:T(8,128)S(1)} %get-tuple-element.8, bf16[64,5,128,128]{3,2,1,0:T(8,128)(2,1)} %param.16, bf16[64,64,128,1]{2,1,0,3:T(8,128)(2,1)S(1)} %bitcast.186), kind=kOutput, calls=%fused_computation.14 | convolution fusion | flops 673710080 | bytes 22021376 | tf_op jit(solution)/shard_map/rsab,nra->rsnb/dot_general | solution.py:42
  292.8 33.0 %scatter_fusion.1 = f32[64,64,128]{2,1,0:T(8,128)S(1)} fusion(f32[64,64,128]{2,1,0:T(8,128)S(1)} %broadcast.76.clone.1, s32[320]{0:T(512)S(1)} %reshape.148, f32[320,64,128]{2,1,0:T(8,128)} %bitcast.182), kind=kCustom, calls=%fused_computation.3 | custom fusion | flops 2621440 | bytes 31458560 | tf_op jit(solution)/shard_map/scatter-add | solution.py:46
  327.1 5.8 cholesky.85
  334.2 4.9 custom-call.17
  339.1 21.5 %reduce-scatter.6.cloned.1.call-done = bf16[64,1024]{1,0:T(8,128)(2,1)} async-done(((bf16[64,8192]{1,0:T(8,128)(2,1)}), bf16[64,1024]{1,0:T(8,128)(2,1)}) %reduce-scatter.6.cloned.1.call-update) | async-done | bytes 131088 | tf_op jit(solution)/shard_map/reduce_scatter | solution.py:65
  361.8 76.1 %all-gather.1 = f32[2048,64]{1,0:T(8,128)S(1)} all-gather(f32[64,64]{1,0:T(8,128)S(1)} %fusion.46), channel_id=3, replica_groups=mesh['row'=8,'col'=4] {'row','col'}, dimensions={0}, use_global_device_ids=true | all-gather | bytes 540672 | tf_op jit(solution)/shard_map/all_gather | solution.py:68
  440.6 20.6 %all-gather.11.cloned.1.call-done = bf16[64,8192]{1,0:T(8,128)(2,1)} async-done(((bf16[64,1024]{1,0:T(8,128)(2,1)}), bf16[64,8192]{1,0:T(8,128)(2,1)}) %all-gather.11.cloned.1.call-update) | async-done | bytes 1048592 | tf_op jit(solution)/shard_map/all_gather | solution.py:74
  462.7 13.3 %gather_fusion.1 = bf16[320,64,128]{2,1,0:T(8,128)(2,1)} fusion(bf16[64,64,128]{2,0,1:T(8,128)(2,1)S(1)} %copy_bitcast_fusion.5, s32[1024]{0:T(1024)S(1)} %pad_clamp_fusion), kind=kCustom, calls=%fused_computation.1.clone | custom fusion | bytes 10487040 | tf_op jit(solution)/shard_map/jit(_take)/gather | solution.py:30
  476.1 11.0 %fusion.11 = bf16[64,8,8,128]{3,2,1,0:T(8,128)(2,1)} fusion(bf16[64,5,128,128]{3,2,1,0:T(8,128)(2,1)} %param.16, bf16[64,5,64,128]{3,2,1,0:T(8,128)(2,1)} %bitcast.183, pred[64,5]{1,0:T(8,128)(4,1)S(1)} %copy.61, bf16[64,5]{1,0:T(8,128)(2,1)S(1)} %get-tuple-element.6), kind=kOutput, calls=%fused_computation.25 | convolution fusion | flops 676855808 | bytes 16778176 | tf_op jit(solution)/shard_map/rsab,nrsb->nra/dot_general | solution.py:31
  487.1 2.6 copy.118
  489.8 52.0 %all-reduce.5.cloned.1.call-done = bf16[64,8192]{1,0:T(8,128)(2,1)} async-done(((bf16[64,8192]{1,0:T(8,128)(2,1)}), bf16[64,8192]{1,0:T(8,128)(2,1)}) %all-reduce.5.cloned.1.call-update) | async-done | bytes 1048592 | tf_op jit(solution)/shard_map/psum | solution.py:76
  543.8 24.4 %psum.31 = f32[64,64]{0,1:T(8,128)S(1)} all-reduce(f32[64,64]{0,1:T(8,128)S(1)} %fusion.47), channel_id=1, replica_groups=mesh['row'=8,'col'=4] {'row'}, use_global_device_ids=true, to_apply=%region_11.16 | all-reduce | flops 4096 | bytes 32768 | tf_op jit(solution)/shard_map/psum | solution.py:77
  568.3 5.8 cholesky.96
  575.5 4.9 custom-call.19
  580.8 2.3 convolution_subtract_fusion
  584.9 10.2 %broadcast_multiply_fusion = f32[64,64,5,128]{3,1,2,0:T(8,128)} fusion(f32[64,5]{1,0:T(8,128)S(1)} %get-tuple-element.8, bf16[64,5,128,128]{3,2,1,0:T(8,128)(2,1)} %param.16, bf16[64,64,128,1]{2,1,0,3:T(8,128)(2,1)S(1)} %bitcast.185), kind=kOutput, calls=%fused_computation.13 | convolution fusion | flops 673710080 | bytes 22021376 | tf_op jit(solution)/shard_map/rsab,nra->rsnb/dot_general | solution.py:42
  595.3 33.0 %scatter_fusion.2 = f32[64,64,128]{2,1,0:T(8,128)S(1)} fusion(f32[64,64,128]{2,1,0:T(8,128)S(1)} %broadcast.76, s32[320]{0:T(512)S(1)} %reshape.148, f32[320,64,128]{2,1,0:T(8,128)} %bitcast.180), kind=kCustom, calls=%fused_computation.4 | custom fusion | flops 2621440 | bytes 31458560 | tf_op jit(solution)/shard_map/scatter-add | solution.py:46
  630.0 5.8 cholesky.107
  637.1 4.9 custom-call.21
  645.0 18.0 %reduce-scatter.8.cloned.1.call-done = bf16[64,1024]{1,0:T(8,128)(2,1)} async-done(((bf16[64,8192]{1,0:T(8,128)(2,1)}), bf16[64,1024]{1,0:T(8,128)(2,1)}) %reduce-scatter.8.cloned.1.call-update) | async-done | bytes 131088 | tf_op jit(solution)/shard_map/reduce_scatter | solution.py:65
  664.2 76.5 %all-gather.2 = f32[2048,64]{1,0:T(8,128)S(1)} all-gather(f32[64,64]{1,0:T(8,128)S(1)} %fusion.48), channel_id=4, replica_groups=mesh['row'=8,'col'=4] {'row','col'}, dimensions={0}, use_global_device_ids=true | all-gather | bytes 540672 | tf_op jit(solution)/shard_map/all_gather | solution.py:68
  (98 shorter events, 42.6 us)
Async XLA Ops:
  7.2 33.7 %all-gather.9.cloned.1.call-start = ((), (), s32[]{:S(2)}) async-start(), calls=%async_computation.5 | async-start | bytes 1310720 | tf_op jit(solution)/shard_map/all_gather | solution.py:58
  9.0 76.8 %all-gather.7.cloned.1.call-start = ((), (), s32[]{:S(2)}) async-start(), calls=%async_computation.3 | async-start | bytes 1179648 | tf_op jit(solution)/shard_map/all_gather | solution.py:74
  10.7 152.7 %all-reduce.3.cloned.1.call-start = ((), (), s32[]{:S(2)}) async-start(), calls=%async_computation.4 | async-start | bytes 2097152 | tf_op jit(solution)/shard_map/psum | solution.py:76
  111.9 167.6 %copy-start.4 = (bf16[64,8192]{1,0:T(8,128)(2,1)S(1)}, bf16[64,8192]{1,0:T(8,128)(2,1)}, u32[]{:S(2)}) copy-start(bf16[64,8192]{1,0:T(8,128)(2,1)} %all-gather.9.cloned.1.call-done) | copy-start | bytes 3145732
  111.9 89.9 %reduce-scatter.4.cloned.1.call-start = ((), (), s32[]{:S(2)}) async-start(), calls=%async_computation.6 | async-start | bytes 1179648 | tf_op jit(solution)/shard_map/reduce_scatter | solution.py:65
  113.1 247.5 %reduce-scatter.6.cloned.1.call-start = ((), (), s32[]{:S(2)}) async-start(), calls=%async_computation.7 | async-start | bytes 1179648 | tf_op jit(solution)/shard_map/reduce_scatter | solution.py:65
  163.4 116.1 %copy-start.3 = (bf16[64,8192]{1,0:T(8,128)(2,1)S(1)}, bf16[64,8192]{1,0:T(8,128)(2,1)}, u32[]{:S(2)}) copy-start(bf16[64,8192]{1,0:T(8,128)(2,1)} %all-reduce.3.cloned.1.call-done) | copy-start | bytes 3145732
  280.6 1.3 copy-start
  325.8 112.6 %copy-start.5 = (f32[64,1024]{1,0:T(8,128)S(1)}, f32[64,1024]{1,0:T(8,128)}, u32[]{:S(2)}) copy-start(f32[64,1024]{1,0:T(8,128)} %param.15) | copy-start | bytes 786436
  326.9 134.3 %all-gather.11.cloned.1.call-start = ((), (), s32[]{:S(2)}) async-start(), calls=%async_computation.8 | async-start | bytes 1179648 | tf_op jit(solution)/shard_map/all_gather | solution.py:74
  440.4 101.4 %all-reduce.5.cloned.1.call-start = ((), (), s32[]{:S(2)}) async-start(), calls=%async_computation.9 | async-start | bytes 2097152 | tf_op jit(solution)/shard_map/psum | solution.py:76
  487.1 93.7 %copy-start.1 = (f32[64,8192]{1,0:T(8,128)S(1)}, f32[64,8192]{1,0:T(8,128)}, u32[]{:S(2)}) copy-start(f32[64,8192]{1,0:T(8,128)} %copy-done) | copy-start | bytes 6291460
  489.7 173.3 %reduce-scatter.8.cloned.1.call-start = ((), (), s32[]{:S(2)}) async-start(), calls=%async_computation.10 | async-start | bytes 1179648 | tf_op jit(solution)/shard_map/reduce_scatter | solution.py:65
  583.1 1.3 copy-start.2
  595.3 34.2 %copy-start.6 = (f32[64,1024]{1,0:T(8,128)S(1)}, f32[64,1024]{1,0:T(8,128)}, u32[]{:S(2)}) copy-start(f32[64,1024]{1,0:T(8,128)} %param.13) | copy-start | bytes 786436
Sparse Core Ops, SparseCore 0:
  10.1 30.6 all-gather.8
  43.3 22.7 all-gather.6
  112.1 51.2 all-reduce.2
  166.4 35.3 reduce-scatter.3
  327.0 33.5 reduce-scatter.5
  440.5 20.6 all-gather.10
  489.9 51.8 all-reduce.4
  629.5 33.4 reduce-scatter.7
